TPU v7x, 512 devices: a whole 4x4x16 slice. The times are simulated.
512 devices in a mesh: elem: 32 (over x_lo, z), band: 16 (over x_hi, y, core).
Axes of the slice: x: 4 (x_hi: 2, x_lo: 2; x = x_hi * 2 + x_lo), y: 4, z: 16, core: 2. Of those that a mesh axis runs over, the one named last changes fastest.
Arguments:
- basis_sizes: int32 [512], P('elem'), may hold values from 96 to 160, as said below
- coupling_pattern: int32 [512], P('elem'), may hold values 0 or 1
- h_diag: bfloat16 [512, 160, 160], P('elem'), may hold values from -0.6708204 to 0.6708204, as said below
- h_couple: bfloat16 [512, 160, 160], P('elem'), may hold values from -0.25 to 0.25
- bands: bfloat16 [1024, 81920], P('band', 'elem'), may hold values from -1500 to 1500
Outputs:
- filtered: bfloat16 [1024, 81920], P('band', 'elem')
Inputs may be any that keep to these rules, and one draw needn't show every extreme that they name: `basis_sizes`: every element has between 96 and 160 basis functions; some element has exactly 160 and some exactly 96. `h_diag`: each block is symmetric.
All inputs are finite; a program needn't handle non-finite values. No bound on the sum of `coupling_pattern` on one device may be relied on, other than what follows from the above.
Results may differ from a plain program's by a relative error of at most 0.0085.
Values may be sent and summed in bfloat16 or wider, within the bound.
A program may use at most 64 MiB of HBM per device.

v0:
```python
import math
import jax
import jax.numpy as jnp
from jax import lax
from jax.sharding import PartitionSpec as P

DEGREE = 6
center_shift = 0.4
half_width = 2.8
epsilon_norm = 1e-06


def from_behind(value, axis, steps):
    count = lax.axis_size(axis)
    pairs = [(source, (source + steps) % count) for source in range(count)]
    return lax.ppermute(value, axis, pairs)


def with_halo(array, sides, width):
    for axis, dim in sides:
        count, length = (lax.axis_size(axis), array.shape[dim])
        up = [(i, (i + 1) % count) for i in range(count)]
        down = [(j, i) for i, j in up]
        last = lax.slice_in_dim(array, length - width, length, axis=dim)
        leading = lax.slice_in_dim(array, 0, width, axis=dim)
        before = lax.ppermute(last, axis, up)
        after = lax.ppermute(leading, axis, down)
        array = jnp.concatenate([before, array, after], axis=dim)
    return array


def cut_along(array, dim, count):
    before, after = (array.shape[:dim], array.shape[dim + 1 :])
    return jnp.moveaxis(array.reshape(*before, count, -1, *after), dim, 0)


def sent_and_summed(array, axis, dim):
    pieces = cut_along(array, dim, lax.axis_size(axis))
    arrived = lax.all_to_all(pieces, axis, split_axis=0, concat_axis=0, tiled=True)
    return arrived.sum(axis=0)


def padded_to(lines, count):
    spare = -len(lines) % count
    return jnp.pad(lines, [(0, spare)] + [(0, 0)] * (lines.ndim - 1))


def in_order(pieces, dim):
    pieces = jnp.moveaxis(pieces, 0, dim)
    dims = pieces.shape
    return pieces.reshape(*dims[:dim], dims[dim] * dims[dim + 1], *dims[dim + 2 :])


def from_everyone(array, axis):
    count = lax.axis_size(axis)
    return lax.all_to_all(
        jnp.broadcast_to(array[None], (count, *array.shape)), axis, 0, 0, tiled=True
    )


def gathered_copies(array, axis, dim):
    return in_order(from_everyone(array, axis), dim)


def nested_sum(array, axes):
    own = sent_and_summed(padded_to(array, lax.axis_size(axes)), axes, 0)
    whole = gathered_copies(own, axes, 0)
    return whole[: len(array)].reshape(array.shape)


def in_one(arrays, axis):
    line, at, done = (jnp.concatenate([a.reshape(-1) for a in arrays]), 0, [])
    running = nested_sum(line, axis)
    for a in arrays:
        done.append(running[at : at + a.size].reshape(a.shape))
        at += a.size
    return tuple(done)


def identity_block(shape, offset):
    row_ids = lax.broadcasted_iota(jnp.int32, shape, 0) + offset
    col_ids = lax.broadcasted_iota(jnp.int32, shape, 1)
    return (row_ids == col_ids).astype(jnp.float32)


def rotation_columns(gram_strip, scales, offset, total_rows):
    own_scales = lax.dynamic_slice_in_dim(scales, offset, gram_strip.shape[0], 0)
    identity = identity_block(gram_strip.shape, offset)
    normed = own_scales[:, None] * gram_strip * scales[None, :]
    return (math.sqrt(total_rows) * scales[None, :] * (1.5 * identity - 0.5 * normed)).astype(
        jnp.bfloat16
    )


def shards(basis_sizes, coupling_pattern, h_diag, h_couple, bands):
    elem_local = h_diag.shape[0]
    basis_width = h_diag.shape[1]
    band_local = bands.shape[0]
    total_rows = elem_local * lax.axis_size("elem") * basis_width
    columns = lax.broadcasted_iota(jnp.int32, (elem_local, basis_width), 1)
    valid_rows = (columns < basis_sizes[:, None]).astype(jnp.float32)
    coupling = h_couple * coupling_pattern.astype(jnp.bfloat16)[:, None, None]
    current = (
        bands.reshape(band_local, elem_local, basis_width) * valid_rows.astype(jnp.bfloat16)[None]
    )
    prior_block = from_behind(coupling[-1], "elem", 1)
    behind = jnp.concatenate([prior_block[None], coupling[:-1]], axis=0)
    previous = current
    for degree in range(DEGREE):
        current_float = current.astype(jnp.float32)
        local_term = jnp.einsum("eij,bej->bei", h_diag, current, preferred_element_type=jnp.float32)
        rimmed = with_halo(current, (("elem", 1),), 1)
        upper_term = jnp.einsum(
            "eij,bej->bei", coupling, rimmed[:, 2:], preferred_element_type=jnp.float32
        )
        lower_term = jnp.einsum(
            "eji,bej->bei", behind, rimmed[:, :-2], preferred_element_type=jnp.float32
        )
        applied = (local_term + upper_term + lower_term) * valid_rows[None]
        shifted = applied - center_shift * current_float
        if degree == 0:
            next_iterate = shifted / half_width
        else:
            next_iterate = 2.0 * shifted / half_width - previous.astype(jnp.float32)
        previous, current = (current, next_iterate.astype(jnp.bfloat16))
    filtered = current.reshape(band_local, elem_local * basis_width)
    every_band = lax.all_gather(filtered, "band", axis=0, tiled=True)
    strip = lax.dot_general(
        filtered, every_band, (((1,), (1,)), ((), ())), preferred_element_type=jnp.float32
    )
    squares = jnp.sum(jnp.square(every_band.astype(jnp.float32)), axis=1)
    strip, squares = in_one((strip, squares), "elem")
    scales = lax.rsqrt(squares + epsilon_norm)
    offset = lax.axis_index("band") * band_local
    weights = rotation_columns(strip, scales, offset, total_rows)
    return jnp.dot(weights, every_band, preferred_element_type=jnp.float32).astype(jnp.bfloat16)


def solution(mesh):
    in_specs = (
        P("elem"),
        P("elem"),
        P("elem", None, None),
        P("elem", None, None),
        P("band", "elem"),
    )
    out_specs = P("band", "elem")
    return jax.shard_map(shards, mesh=mesh, in_specs=in_specs, out_specs=out_specs, check_vma=False)
```

profile of v0, /device:TPU:4, one launch (start us, length us, event | category | flops | bytes accessed | tf_op | source)
XLA Modules:
  0.0 235.6 jit_solution(5489966992753871043)
XLA Ops:
  6.5 0.9 fusion.79
  7.4 1.6 reshape.59
  9.0 0.2 copy_multiply_fusion
  9.2 3.8 %collective-permute-start.1 = (bf16[64,1,160]{2,0,1:T(8,128)(2,1)S(1)}, bf16[64,1,160]{2,0,1:T(8,128)(2,1)S(1)}, u32[]{:S(2)}, u32[]{:S(2)}) collective-permute-start(bf16[64,1,160]{2,0,1:T(8,128)(2,1)S(1)} %get-tuple-element.15), channel_id=1, source_target_pairs={{0,16},{16,32},{32,48},{48,64},{64,80},{80,96},{96,112},{112,128},... | collective-permute-start | bytes 61448 | tf_op jit(solution)/shard_map/ppermute | solution.py:26
  13.0 10.1 %collective-permute-start = (bf16[64,1,160]{2,0,1:T(8,128)(2,1)S(1)}, bf16[64,1,160]{2,0,1:T(8,128)(2,1)S(1)}, u32[]{:S(2)}, u32[]{:S(2)}) collective-permute-start(bf16[64,1,160]{2,0,1:T(8,128)(2,1)S(1)} %get-tuple-element.16), channel_id=1, source_target_pairs={{16,0},{32,16},{48,32},{64,48},{80,64},{96,80},{112,96},{128,112},... | collective-permute-start | bytes 61448 | tf_op jit(solution)/shard_map/ppermute | solution.py:27
  23.2 0.2 broadcast_multiply_fusion
  23.4 1.9 collective-permute-start.2
  25.3 0.6 fusion.103
  25.9 0.1 slice.131
  26.0 0.0 collective-permute-done
  26.0 0.5 convolution_add_fusion.11
  26.5 0.0 collective-permute-done.1
  26.5 5.3 %collective-permute-done.2 = bf16[160,160]{1,0:T(8,128)(2,1)S(1)} collective-permute-done((bf16[160,160]{1,0:T(8,128)(2,1)S(1)}, bf16[160,160]{1,0:T(8,128)(2,1)S(1)}, u32[]{:S(2)}, u32[]{:S(2)}) %collective-permute-start.2) | collective-permute-done | bytes 51232 | tf_op jit(solution)/shard_map/ppermute | solution.py:16
  31.8 0.4 fusion.24
  32.3 1.9 collective-permute-start.3
  34.2 0.6 fusion.104
  34.8 3.9 %collective-permute-start.4 = (bf16[64,1,160]{2,0,1:T(8,128)(2,1)S(1)}, bf16[64,1,160]{2,0,1:T(8,128)(2,1)S(1)}, u32[]{:S(2)}, u32[]{:S(2)}) collective-permute-start(bf16[64,1,160]{2,0,1:T(8,128)(2,1)S(1)} %get-tuple-element.13), channel_id=1, source_target_pairs={{0,16},{16,32},{32,48},{48,64},{64,80},{80,96},{96,112},{112,128},... | collective-permute-start | bytes 61448 | tf_op jit(solution)/shard_map/ppermute | solution.py:26
  38.7 0.0 collective-permute-done.3
  38.7 0.5 convolution_add_fusion.9
  39.3 3.4 %collective-permute-done.4 = bf16[64,1,160]{2,0,1:T(8,128)(2,1)S(1)} collective-permute-done((bf16[64,1,160]{2,0,1:T(8,128)(2,1)S(1)}, bf16[64,1,160]{2,0,1:T(8,128)(2,1)S(1)}, u32[]{:S(2)}, u32[]{:S(2)}) %collective-permute-start.4) | collective-permute-done | bytes 20512 | tf_op jit(solution)/shard_map/ppermute | solution.py:26
  42.7 0.5 fusion.25
  43.2 1.9 collective-permute-start.5
  45.2 0.6 fusion.105
  45.7 3.9 %collective-permute-start.6 = (bf16[64,1,160]{2,0,1:T(8,128)(2,1)S(1)}, bf16[64,1,160]{2,0,1:T(8,128)(2,1)S(1)}, u32[]{:S(2)}, u32[]{:S(2)}) collective-permute-start(bf16[64,1,160]{2,0,1:T(8,128)(2,1)S(1)} %get-tuple-element.11), channel_id=1, source_target_pairs={{0,16},{16,32},{32,48},{48,64},{64,80},{80,96},{96,112},{112,128},... | collective-permute-start | bytes 61448 | tf_op jit(solution)/shard_map/ppermute | solution.py:26
  49.6 0.0 collective-permute-done.5
  49.7 0.5 convolution_add_fusion.7
  50.2 3.4 %collective-permute-done.6 = bf16[64,1,160]{2,0,1:T(8,128)(2,1)S(1)} collective-permute-done((bf16[64,1,160]{2,0,1:T(8,128)(2,1)S(1)}, bf16[64,1,160]{2,0,1:T(8,128)(2,1)S(1)}, u32[]{:S(2)}, u32[]{:S(2)}) %collective-permute-start.6) | collective-permute-done | bytes 20512 | tf_op jit(solution)/shard_map/ppermute | solution.py:26
  53.6 0.5 fusion.26
  54.2 1.9 collective-permute-start.7
  56.1 0.6 fusion.106
  56.6 3.9 %collective-permute-start.8 = (bf16[64,1,160]{2,0,1:T(8,128)(2,1)S(1)}, bf16[64,1,160]{2,0,1:T(8,128)(2,1)S(1)}, u32[]{:S(2)}, u32[]{:S(2)}) collective-permute-start(bf16[64,1,160]{2,0,1:T(8,128)(2,1)S(1)} %get-tuple-element.9), channel_id=1, source_target_pairs={{0,16},{16,32},{32,48},{48,64},{64,80},{80,96},{96,112},{112,128},... | collective-permute-start | bytes 61448 | tf_op jit(solution)/shard_map/ppermute | solution.py:26
  60.6 0.5 convolution_add_fusion.5
  61.1 3.4 %collective-permute-done.8 = bf16[64,1,160]{2,0,1:T(8,128)(2,1)S(1)} collective-permute-done((bf16[64,1,160]{2,0,1:T(8,128)(2,1)S(1)}, bf16[64,1,160]{2,0,1:T(8,128)(2,1)S(1)}, u32[]{:S(2)}, u32[]{:S(2)}) %collective-permute-start.8) | collective-permute-done | bytes 20512 | tf_op jit(solution)/shard_map/ppermute | solution.py:26
  64.6 0.5 fusion.27
  65.1 1.9 collective-permute-start.9
  67.0 0.6 fusion.107
  67.6 3.9 %collective-permute-start.10 = (bf16[64,1,160]{2,0,1:T(8,128)(2,1)S(1)}, bf16[64,1,160]{2,0,1:T(8,128)(2,1)S(1)}, u32[]{:S(2)}, u32[]{:S(2)}) collective-permute-start(bf16[64,1,160]{2,0,1:T(8,128)(2,1)S(1)} %get-tuple-element.7), channel_id=1, source_target_pairs={{0,16},{16,32},{32,48},{48,64},{64,80},{80,96},{96,112},{112,128},... | collective-permute-start | bytes 61448 | tf_op jit(solution)/shard_map/ppermute | solution.py:26
  71.5 0.0 collective-permute-done.9
  71.5 0.5 convolution_add_fusion.3
  72.0 3.4 %collective-permute-done.10 = bf16[64,1,160]{2,0,1:T(8,128)(2,1)S(1)} collective-permute-done((bf16[64,1,160]{2,0,1:T(8,128)(2,1)S(1)}, bf16[64,1,160]{2,0,1:T(8,128)(2,1)S(1)}, u32[]{:S(2)}, u32[]{:S(2)}) %collective-permute-start.10) | collective-permute-done | bytes 20512 | tf_op jit(solution)/shard_map/ppermute | solution.py:26
  75.5 0.5 fusion.28
  76.0 1.9 collective-permute-start.11
  77.9 0.6 fusion.108
  78.5 4.1 %collective-permute-start.12 = (bf16[64,1,160]{2,0,1:T(8,128)(2,1)S(1)}, bf16[64,1,160]{2,0,1:T(8,128)(2,1)S(1)}, u32[]{:S(2)}, u32[]{:S(2)}) collective-permute-start(bf16[64,1,160]{2,0,1:T(8,128)(2,1)S(1)} %get-tuple-element.5), channel_id=1, source_target_pairs={{0,16},{16,32},{32,48},{48,64},{64,80},{80,96},{96,112},{112,128},... | collective-permute-start | bytes 61448 | tf_op jit(solution)/shard_map/ppermute | solution.py:26
  82.6 0.5 convolution_add_fusion.1
  83.1 3.3 %collective-permute-done.12 = bf16[64,1,160]{2,0,1:T(8,128)(2,1)S(1)} collective-permute-done((bf16[64,1,160]{2,0,1:T(8,128)(2,1)S(1)}, bf16[64,1,160]{2,0,1:T(8,128)(2,1)S(1)}, u32[]{:S(2)}, u32[]{:S(2)}) %collective-permute-start.12) | collective-permute-done | bytes 20512 | tf_op jit(solution)/shard_map/ppermute | solution.py:26
  86.4 0.5 fusion.29
  86.9 0.3 copy.11
  87.2 1.5 reshape.60
  88.7 0.0 all-gather.2.cloned.1.call-update
  88.7 64.4 %all-gather.2.cloned.1.call-done = bf16[1024,2560]{1,0:T(8,128)(2,1)} async-done(((bf16[64,2560]{1,0:T(8,128)(2,1)}), bf16[1024,2560]{1,0:T(8,128)(2,1)}) %all-gather.2.cloned.1.call-update) | async-done | bytes 5242896 | tf_op jit(solution)/shard_map/all_gather | solution.py:127
  153.1 4.4 %convolution_bitcast_fusion = f32[8,8,8,128]{3,2,1,0:T(8,128)S(1)} fusion(bf16[64,2560]{1,0:T(8,128)(2,1)} %reshape.60, bf16[1024,2560]{1,0:T(8,128)(2,1)} %all-gather.2.cloned.1.call-done), kind=kOutput, calls=%fused_computation.55 | convolution fusion | flops 335544320 | bytes 5832704 | tf_op jit(solution)/shard_map/dot_general | solution.py:128
  157.6 1.1 multiply_reduce_fusion
  158.7 0.4 all_to_all.10
  159.1 37.1 %all_to_all.15 = f32[32,1,2080]{2,1,0:T(1,128)S(1)} all-to-all(f32[32,1,2080]{2,1,0:T(1,128)S(1)} %all_to_all.10), channel_id=1, replica_groups=mesh['elem'=32,'band'=16] {'elem'}, dimensions={0} | all-to-all | bytes 532480 | tf_op jit(solution)/shard_map/all_to_all | solution.py:39
  196.1 0.2 reduce_sum.19
  196.3 0.9 broadcast_in_dim.5
  197.1 3.9 %all-to-all-start.1 = ((f32[32,1,2080]{2,1,0:T(1,128)}), f32[32,1,2080]{2,1,0:T(1,128)S(1)}, u32[]{:S(2)}, u32[]{:S(2)}) async-start(f32[32,1,2080]{2,1,0:T(1,128)} %broadcast_in_dim.5), calls=%async_computation.1 | async-start | bytes 557056 | tf_op jit(solution)/shard_map/all_to_all | solution.py:56
  201.0 22.1 %all-to-all-done.1 = f32[32,1,2080]{2,1,0:T(1,128)S(1)} async-done(((f32[32,1,2080]{2,1,0:T(1,128)}), f32[32,1,2080]{2,1,0:T(1,128)S(1)}, u32[]{:S(2)}, u32[]{:S(2)}) %all-to-all-start.1) | async-done | bytes 266272 | tf_op jit(solution)/shard_map/all_to_all | solution.py:56
  223.2 0.7 reduce.1
  223.8 0.2 reshape.62
  224.1 0.3 slice.126
  224.3 0.1 dynamic_slice.3
  224.4 4.3 %convolution_convert_fusion = bf16[64,2560]{1,0:T(8,128)(2,1)} fusion(bf16[1024,2560]{1,0:T(8,128)(2,1)} %all-gather.2.cloned.1.call-done, f32[65,1024]{1,0:T(8,128)S(1)} %slice.126, f32[1024]{0:T(1024)S(1)} %get-tuple-element.18, f32[64]{0:T(128)S(1)} %dynamic_slice.3, s32[64]{0:T(128)S(1)} %iota_add_fusion, f32[1024]{0:T(1024)S(1)} %get-tuple-element.17), kind=kOutput, calls=%fused_computation.1 | convolution fusion | flops 336232448 | bytes 5841920 | tf_op jit(solution)/shard_map/dot_general | solution.py:136
  (23 shorter events, 0.2 us)
Async XLA Ops:
  6.5 18.8 %copy-start = (bf16[16,160,160]{2,1,0:T(8,128)(2,1)S(1)}, bf16[16,160,160]{2,1,0:T(8,128)(2,1)}, u32[]{:S(2)}) copy-start(bf16[16,160,160]{2,1,0:T(8,128)(2,1)} %param.7) | copy-start | bytes 2457604
  6.5 16.7 %copy-start.3 = (s32[16]{0:T(128)S(1)}, s32[16]{0:T(128)}, u32[]{:S(2)}) copy-start(s32[16]{0:T(128)} %param.6) | copy-start | bytes 196
  6.5 16.7 %copy-start.2 = (bf16[16,160,160]{2,1,0:T(8,128)(2,1)S(1)}, bf16[16,160,160]{2,1,0:T(8,128)(2,1)}, u32[]{:S(2)}) copy-start(bf16[16,160,160]{2,1,0:T(8,128)(2,1)} %param.8) | copy-start | bytes 2457604
  6.5 146.5 %all-gather.2.cloned.1.call-start = ((), (), s32[]{:S(2)}) async-start(), calls=%async_computation.2 | async-start | bytes 5570560 | tf_op jit(solution)/shard_map/all_gather | solution.py:127
  9.2 17.3 %collective-permute-start.1 = (bf16[64,1,160]{2,0,1:T(8,128)(2,1)S(1)}, bf16[64,1,160]{2,0,1:T(8,128)(2,1)S(1)}, u32[]{:S(2)}, u32[]{:S(2)}) collective-permute-start(bf16[64,1,160]{2,0,1:T(8,128)(2,1)S(1)} %get-tuple-element.15), channel_id=1, source_target_pairs={{0,16},{16,32},{32,48},{48,64},{64,80},{80,96},{96,112},{112,128},... | collective-permute-start | bytes 61448 | tf_op jit(solution)/shard_map/ppermute | solution.py:26
  13.0 12.9 %collective-permute-start = (bf16[64,1,160]{2,0,1:T(8,128)(2,1)S(1)}, bf16[64,1,160]{2,0,1:T(8,128)(2,1)S(1)}, u32[]{:S(2)}, u32[]{:S(2)}) collective-permute-start(bf16[64,1,160]{2,0,1:T(8,128)(2,1)S(1)} %get-tuple-element.16), channel_id=1, source_target_pairs={{16,0},{32,16},{48,32},{64,48},{80,64},{96,80},{112,96},{128,112},... | collective-permute-start | bytes 61448 | tf_op jit(solution)/shard_map/ppermute | solution.py:27
  23.4 8.4 %collective-permute-start.2 = (bf16[160,160]{1,0:T(8,128)(2,1)S(1)}, bf16[160,160]{1,0:T(8,128)(2,1)S(1)}, u32[]{:S(2)}, u32[]{:S(2)}) collective-permute-start(bf16[160,160]{1,0:T(8,128)(2,1)S(1)} %slice_bitcast_fusion), channel_id=1, source_target_pairs={{0,16},{16,32},{32,48},{48,64},{64,80},{80,96},{96,112},{112,128},... | collective-permute-start | bytes 153608 | tf_op jit(solution)/shard_map/ppermute | solution.py:16
  32.3 6.4 %collective-permute-start.3 = (bf16[64,1,160]{2,0,1:T(8,128)(2,1)S(1)}, bf16[64,1,160]{2,0,1:T(8,128)(2,1)S(1)}, u32[]{:S(2)}, u32[]{:S(2)}) collective-permute-start(bf16[64,1,160]{2,0,1:T(8,128)(2,1)S(1)} %get-tuple-element.14), channel_id=1, source_target_pairs={{16,0},{32,16},{48,32},{64,48},{80,64},{96,80},{112,96},{128,112},... | collective-permute-start | bytes 61448 | tf_op jit(solution)/shard_map/ppermute | solution.py:27
  34.8 7.9 %collective-permute-start.4 = (bf16[64,1,160]{2,0,1:T(8,128)(2,1)S(1)}, bf16[64,1,160]{2,0,1:T(8,128)(2,1)S(1)}, u32[]{:S(2)}, u32[]{:S(2)}) collective-permute-start(bf16[64,1,160]{2,0,1:T(8,128)(2,1)S(1)} %get-tuple-element.13), channel_id=1, source_target_pairs={{0,16},{16,32},{32,48},{48,64},{64,80},{80,96},{96,112},{112,128},... | collective-permute-start | bytes 61448 | tf_op jit(solution)/shard_map/ppermute | solution.py:26
  43.2 6.4 %collective-permute-start.5 = (bf16[64,1,160]{2,0,1:T(8,128)(2,1)S(1)}, bf16[64,1,160]{2,0,1:T(8,128)(2,1)S(1)}, u32[]{:S(2)}, u32[]{:S(2)}) collective-permute-start(bf16[64,1,160]{2,0,1:T(8,128)(2,1)S(1)} %get-tuple-element.12), channel_id=1, source_target_pairs={{16,0},{32,16},{48,32},{64,48},{80,64},{96,80},{112,96},{128,112},... | collective-permute-start | bytes 61448 | tf_op jit(solution)/shard_map/ppermute | solution.py:27
  45.7 7.9 %collective-permute-start.6 = (bf16[64,1,160]{2,0,1:T(8,128)(2,1)S(1)}, bf16[64,1,160]{2,0,1:T(8,128)(2,1)S(1)}, u32[]{:S(2)}, u32[]{:S(2)}) collective-permute-start(bf16[64,1,160]{2,0,1:T(8,128)(2,1)S(1)} %get-tuple-element.11), channel_id=1, source_target_pairs={{0,16},{16,32},{32,48},{48,64},{64,80},{80,96},{96,112},{112,128},... | collective-permute-start | bytes 61448 | tf_op jit(solution)/shard_map/ppermute | solution.py:26
  54.2 6.4 %collective-permute-start.7 = (bf16[64,1,160]{2,0,1:T(8,128)(2,1)S(1)}, bf16[64,1,160]{2,0,1:T(8,128)(2,1)S(1)}, u32[]{:S(2)}, u32[]{:S(2)}) collective-permute-start(bf16[64,1,160]{2,0,1:T(8,128)(2,1)S(1)} %get-tuple-element.10), channel_id=1, source_target_pairs={{16,0},{32,16},{48,32},{64,48},{80,64},{96,80},{112,96},{128,112},... | collective-permute-start | bytes 61448 | tf_op jit(solution)/shard_map/ppermute | solution.py:27
  56.6 7.9 %collective-permute-start.8 = (bf16[64,1,160]{2,0,1:T(8,128)(2,1)S(1)}, bf16[64,1,160]{2,0,1:T(8,128)(2,1)S(1)}, u32[]{:S(2)}, u32[]{:S(2)}) collective-permute-start(bf16[64,1,160]{2,0,1:T(8,128)(2,1)S(1)} %get-tuple-element.9), channel_id=1, source_target_pairs={{0,16},{16,32},{32,48},{48,64},{64,80},{80,96},{96,112},{112,128},... | collective-permute-start | bytes 61448 | tf_op jit(solution)/shard_map/ppermute | solution.py:26
  65.1 6.4 %collective-permute-start.9 = (bf16[64,1,160]{2,0,1:T(8,128)(2,1)S(1)}, bf16[64,1,160]{2,0,1:T(8,128)(2,1)S(1)}, u32[]{:S(2)}, u32[]{:S(2)}) collective-permute-start(bf16[64,1,160]{2,0,1:T(8,128)(2,1)S(1)} %get-tuple-element.8), channel_id=1, source_target_pairs={{16,0},{32,16},{48,32},{64,48},{80,64},{96,80},{112,96},{128,112},... | collective-permute-start | bytes 61448 | tf_op jit(solution)/shard_map/ppermute | solution.py:27
  67.6 7.9 %collective-permute-start.10 = (bf16[64,1,160]{2,0,1:T(8,128)(2,1)S(1)}, bf16[64,1,160]{2,0,1:T(8,128)(2,1)S(1)}, u32[]{:S(2)}, u32[]{:S(2)}) collective-permute-start(bf16[64,1,160]{2,0,1:T(8,128)(2,1)S(1)} %get-tuple-element.7), channel_id=1, source_target_pairs={{0,16},{16,32},{32,48},{48,64},{64,80},{80,96},{96,112},{112,128},... | collective-permute-start | bytes 61448 | tf_op jit(solution)/shard_map/ppermute | solution.py:26
  76.0 6.6 %collective-permute-start.11 = (bf16[64,1,160]{2,0,1:T(8,128)(2,1)S(1)}, bf16[64,1,160]{2,0,1:T(8,128)(2,1)S(1)}, u32[]{:S(2)}, u32[]{:S(2)}) collective-permute-start(bf16[64,1,160]{2,0,1:T(8,128)(2,1)S(1)} %get-tuple-element.6), channel_id=1, source_target_pairs={{16,0},{32,16},{48,32},{64,48},{80,64},{96,80},{112,96},{128,112},... | collective-permute-start | bytes 61448 | tf_op jit(solution)/shard_map/ppermute | solution.py:27
  78.5 7.9 %collective-permute-start.12 = (bf16[64,1,160]{2,0,1:T(8,128)(2,1)S(1)}, bf16[64,1,160]{2,0,1:T(8,128)(2,1)S(1)}, u32[]{:S(2)}, u32[]{:S(2)}) collective-permute-start(bf16[64,1,160]{2,0,1:T(8,128)(2,1)S(1)} %get-tuple-element.5), channel_id=1, source_target_pairs={{0,16},{16,32},{32,48},{48,64},{64,80},{80,96},{96,112},{112,128},... | collective-permute-start | bytes 61448 | tf_op jit(solution)/shard_map/ppermute | solution.py:26
  153.1 4.5 %copy-start.1 = (bf16[1024,2560]{1,0:T(8,128)(2,1)S(1)}, bf16[1024,2560]{1,0:T(8,128)(2,1)}, u32[]{:S(2)}) copy-start(bf16[1024,2560]{1,0:T(8,128)(2,1)} %all-gather.2.cloned.1.call-done) | copy-start | bytes 15728644
  197.1 26.0 %all-to-all-start.1 = ((f32[32,1,2080]{2,1,0:T(1,128)}), f32[32,1,2080]{2,1,0:T(1,128)S(1)}, u32[]{:S(2)}, u32[]{:S(2)}) async-start(f32[32,1,2080]{2,1,0:T(1,128)} %broadcast_in_dim.5), calls=%async_computation.1 | async-start | bytes 557056 | tf_op jit(solution)/shard_map/all_to_all | solution.py:56
Sparse Core Ops, SparseCore 0:
  88.8 64.1 all-gather.1
where the time goes:
time: 236 us
  waiting for transfers between devices  109 us (46%)
  starting transfers between devices  49.1 us (21%)
  blocking collectives  37.1 us (16%)
  matrix products  18.3 us (8%)
  between operations  13.8 us (6%)
  local copies, waits for them, and re-layouts  5.35 us (2%)
  other arithmetic  3.15 us (1%)
    all_gather x1, waiting for transfers between devices, shards(): every_band = lax.all_gather(filtered, 'band', axis=0, tiled=True)  64.4 us
    all_to_all x1, blocking collectives, sent_and_summed(): lax.all_to_all(pieces, axis, split_axis=0, concat_axis=0, tiled=True)  37.1 us
    ppermute x6, starting transfers between devices, with_halo(): before = lax.ppermute(last, axis, up)  23.6 us
    all_to_all x1, waiting for transfers between devices, from_everyone(): lax.all_to_all(jnp.broadcast_to(array[None], (count, *array.shape)), axis...  22.1 us
    ppermute x6, starting transfers between devices, with_halo(): after = lax.ppermute(leading, axis, down)  19.7 us
    ppermute x6, waiting for transfers between devices, with_halo(): before = lax.ppermute(last, axis, up)  17 us
    ppermute x1, waiting for transfers between devices, from_behind(): return lax.ppermute(value, axis, pairs)  5.3 us
  transfers between devices with their start and end apart: 15, of which 8 were waited for; matrix products, arithmetic and copies ran while one was open for 3% of the time, Pallas kernels for 0%

commit v1 on v0

--- a/solution.py
+++ b/solution.py
@@ -124,7 +124,9 @@
             next_iterate = 2.0 * shifted / half_width - previous.astype(jnp.float32)
         previous, current = (current, next_iterate.astype(jnp.bfloat16))
     filtered = current.reshape(band_local, elem_local * basis_width)
-    every_band = lax.all_gather(filtered, "band", axis=0, tiled=True)
+    every_band = jnp.concatenate(
+        lax.all_to_all(jnp.stack([filtered] * lax.axis_size("band")), "band", 0, 0), axis=0
+    )
     strip = lax.dot_general(
         filtered, every_band, (((1,), (1,)), ((), ())), preferred_element_type=jnp.float32
     )

time: 236 us -> 215 us (0.911)
  the two profiles are of different devices: /device:TPU:4 before, /device:TPU:24 now
where the time goes in v1:
time: 215 us; the launch traced here: 214 us
  blocking collectives  94.1 us (44%)
  starting transfers between devices  49.2 us (23%)
  waiting for transfers between devices  46.1 us (21%)
  matrix products  15.5 us (7%)
  local copies, waits for them, and re-layouts  5.74 us (3%)
  other arithmetic  3.15 us (1%)
    all_to_all x1, blocking collectives, shards(): lax.all_to_all(jnp.stack([filtered] * lax.axis_size('band')), 'band', 0, 0)  67.4 us
    all_to_all x1, blocking collectives, sent_and_summed(): lax.all_to_all(pieces, axis, split_axis=0, concat_axis=0, tiled=True)  26.7 us
    ppermute x6, starting transfers between devices, with_halo(): after = lax.ppermute(leading, axis, down)  23.9 us
    ppermute x6, waiting for transfers between devices, with_halo(): before = lax.ppermute(last, axis, up)  23.9 us
    all_to_all x1, waiting for transfers between devices, from_everyone(): lax.all_to_all(jnp.broadcast_to(array[None], (count, *array.shape)), axis...  22.2 us
    ppermute x6, starting transfers between devices, with_halo(): before = lax.ppermute(last, axis, up)  19.5 us
    dot_general x1, matrix products, shards(): jnp.dot(weights, every_band, preferred_element_type=jnp.float32)  4.31 us
  transfers between devices with their start and end apart: 14, of which 7 were waited for; matrix products, arithmetic and copies ran while one was open for 3% of the time, Pallas kernels for 0%

profile of v1, /device:TPU:24, one launch (start us, length us, event | category | flops | bytes accessed | tf_op | source)
XLA Modules:
  0.0 214.3 jit_solution(16017049923737742627)
XLA Ops:
  0.0 0.9 fusion.79
  0.9 1.6 reshape.65
  2.5 0.2 copy_multiply_fusion
  2.7 12.3 %collective-permute-start = (bf16[64,1,160]{2,0,1:T(8,128)(2,1)S(1)}, bf16[64,1,160]{2,0,1:T(8,128)(2,1)S(1)}, u32[]{:S(2)}, u32[]{:S(2)}) collective-permute-start(bf16[64,1,160]{2,0,1:T(8,128)(2,1)S(1)} %get-tuple-element.16), channel_id=1, source_target_pairs={{16,0},{32,16},{48,32},{64,48},{80,64},{96,80},{112,96},{128,112},... | collective-permute-start | bytes 61448 | tf_op jit(solution)/shard_map/ppermute | solution.py:27
  15.0 0.2 broadcast_multiply_fusion
  15.2 1.9 collective-permute-start.2
  17.2 1.9 collective-permute-start.1
  19.1 0.6 fusion.103
  19.6 0.1 slice.131
  19.7 0.5 convolution_add_fusion.11
  20.3 4.8 %collective-permute-done.1 = bf16[64,1,160]{2,0,1:T(8,128)(2,1)S(1)} collective-permute-done((bf16[64,1,160]{2,0,1:T(8,128)(2,1)S(1)}, bf16[64,1,160]{2,0,1:T(8,128)(2,1)S(1)}, u32[]{:S(2)}, u32[]{:S(2)}) %collective-permute-start.1) | collective-permute-done | bytes 20512 | tf_op jit(solution)/shard_map/ppermute | solution.py:26
  25.1 0.0 collective-permute-done.2
  25.1 0.4 fusion.24
  25.5 3.9 %collective-permute-start.3 = (bf16[64,1,160]{2,0,1:T(8,128)(2,1)S(1)}, bf16[64,1,160]{2,0,1:T(8,128)(2,1)S(1)}, u32[]{:S(2)}, u32[]{:S(2)}) collective-permute-start(bf16[64,1,160]{2,0,1:T(8,128)(2,1)S(1)} %get-tuple-element.14), channel_id=1, source_target_pairs={{16,0},{32,16},{48,32},{64,48},{80,64},{96,80},{112,96},{128,112},... | collective-permute-start | bytes 61448 | tf_op jit(solution)/shard_map/ppermute | solution.py:27
  29.5 0.6 fusion.104
  30.0 1.9 collective-permute-start.4
  31.9 0.0 collective-permute-done.3
  32.0 0.5 convolution_add_fusion.9
  32.5 5.4 %collective-permute-done.4 = bf16[64,1,160]{2,0,1:T(8,128)(2,1)S(1)} collective-permute-done((bf16[64,1,160]{2,0,1:T(8,128)(2,1)S(1)}, bf16[64,1,160]{2,0,1:T(8,128)(2,1)S(1)}, u32[]{:S(2)}, u32[]{:S(2)}) %collective-permute-start.4) | collective-permute-done | bytes 20512 | tf_op jit(solution)/shard_map/ppermute | solution.py:26
  37.9 0.5 fusion.25
  38.5 1.9 collective-permute-start.5
  40.4 0.6 fusion.105
  40.9 3.9 %collective-permute-start.6 = (bf16[64,1,160]{2,0,1:T(8,128)(2,1)S(1)}, bf16[64,1,160]{2,0,1:T(8,128)(2,1)S(1)}, u32[]{:S(2)}, u32[]{:S(2)}) collective-permute-start(bf16[64,1,160]{2,0,1:T(8,128)(2,1)S(1)} %get-tuple-element.11), channel_id=1, source_target_pairs={{0,16},{16,32},{32,48},{48,64},{64,80},{80,96},{96,112},{112,128},... | collective-permute-start | bytes 61448 | tf_op jit(solution)/shard_map/ppermute | solution.py:26
  44.9 0.5 convolution_add_fusion.7
  45.4 3.4 %collective-permute-done.6 = bf16[64,1,160]{2,0,1:T(8,128)(2,1)S(1)} collective-permute-done((bf16[64,1,160]{2,0,1:T(8,128)(2,1)S(1)}, bf16[64,1,160]{2,0,1:T(8,128)(2,1)S(1)}, u32[]{:S(2)}, u32[]{:S(2)}) %collective-permute-start.6) | collective-permute-done | bytes 20512 | tf_op jit(solution)/shard_map/ppermute | solution.py:26
  48.9 0.5 fusion.26
  49.4 1.9 collective-permute-start.7
  51.3 0.6 fusion.106
  51.9 3.9 %collective-permute-start.8 = (bf16[64,1,160]{2,0,1:T(8,128)(2,1)S(1)}, bf16[64,1,160]{2,0,1:T(8,128)(2,1)S(1)}, u32[]{:S(2)}, u32[]{:S(2)}) collective-permute-start(bf16[64,1,160]{2,0,1:T(8,128)(2,1)S(1)} %get-tuple-element.9), channel_id=1, source_target_pairs={{0,16},{16,32},{32,48},{48,64},{64,80},{80,96},{96,112},{112,128},... | collective-permute-start | bytes 61448 | tf_op jit(solution)/shard_map/ppermute | solution.py:26
  55.8 0.5 convolution_add_fusion.5
  56.3 3.4 %collective-permute-done.8 = bf16[64,1,160]{2,0,1:T(8,128)(2,1)S(1)} collective-permute-done((bf16[64,1,160]{2,0,1:T(8,128)(2,1)S(1)}, bf16[64,1,160]{2,0,1:T(8,128)(2,1)S(1)}, u32[]{:S(2)}, u32[]{:S(2)}) %collective-permute-start.8) | collective-permute-done | bytes 20512 | tf_op jit(solution)/shard_map/ppermute | solution.py:26
  59.8 0.5 fusion.27
  60.3 1.9 collective-permute-start.9
  62.2 0.6 fusion.107
  62.8 3.9 %collective-permute-start.10 = (bf16[64,1,160]{2,0,1:T(8,128)(2,1)S(1)}, bf16[64,1,160]{2,0,1:T(8,128)(2,1)S(1)}, u32[]{:S(2)}, u32[]{:S(2)}) collective-permute-start(bf16[64,1,160]{2,0,1:T(8,128)(2,1)S(1)} %get-tuple-element.7), channel_id=1, source_target_pairs={{0,16},{16,32},{32,48},{48,64},{64,80},{80,96},{96,112},{112,128},... | collective-permute-start | bytes 61448 | tf_op jit(solution)/shard_map/ppermute | solution.py:26
  66.7 0.5 convolution_add_fusion.3
  67.3 3.4 %collective-permute-done.10 = bf16[64,1,160]{2,0,1:T(8,128)(2,1)S(1)} collective-permute-done((bf16[64,1,160]{2,0,1:T(8,128)(2,1)S(1)}, bf16[64,1,160]{2,0,1:T(8,128)(2,1)S(1)}, u32[]{:S(2)}, u32[]{:S(2)}) %collective-permute-start.10) | collective-permute-done | bytes 20512 | tf_op jit(solution)/shard_map/ppermute | solution.py:26
  70.7 0.5 fusion.28
  71.2 1.9 collective-permute-start.11
  73.1 0.6 fusion.108
  73.7 3.9 %collective-permute-start.12 = (bf16[64,1,160]{2,0,1:T(8,128)(2,1)S(1)}, bf16[64,1,160]{2,0,1:T(8,128)(2,1)S(1)}, u32[]{:S(2)}, u32[]{:S(2)}) collective-permute-start(bf16[64,1,160]{2,0,1:T(8,128)(2,1)S(1)} %get-tuple-element.5), channel_id=1, source_target_pairs={{0,16},{16,32},{32,48},{48,64},{64,80},{80,96},{96,112},{112,128},... | collective-permute-start | bytes 61448 | tf_op jit(solution)/shard_map/ppermute | solution.py:26
  77.6 0.5 convolution_add_fusion.1
  78.2 3.4 %collective-permute-done.12 = bf16[64,1,160]{2,0,1:T(8,128)(2,1)S(1)} collective-permute-done((bf16[64,1,160]{2,0,1:T(8,128)(2,1)S(1)}, bf16[64,1,160]{2,0,1:T(8,128)(2,1)S(1)}, u32[]{:S(2)}, u32[]{:S(2)}) %collective-permute-start.12) | collective-permute-done | bytes 20512 | tf_op jit(solution)/shard_map/ppermute | solution.py:26
  81.6 0.5 fusion.29
  82.1 0.3 copy.11
  82.4 0.7 reshape.66
  83.2 0.5 stack.3
  83.7 67.4 %all_to_all.20 = bf16[16,64,2560]{2,1,0:T(8,128)(2,1)S(1)} all-to-all(bf16[16,64,2560]{2,1,0:T(8,128)(2,1)S(1)} %stack.3), channel_id=1, replica_groups=mesh['elem'=32,'band'=16] {'band'}, dimensions={0} | all-to-all | bytes 10485760 | tf_op jit(solution)/shard_map/all_to_all | solution.py:128
  151.1 1.7 convolution_bitcast_fusion
  152.8 0.1 copy.14
  152.8 0.6 copy-done.1
  153.4 1.1 multiply_reduce_fusion
  154.5 0.1 reduce_sum.21
  154.6 0.4 all_to_all.14
  155.0 26.7 %all_to_all.21 = f32[32,1,2080]{2,1,0:T(1,128)S(1)} all-to-all(f32[32,1,2080]{2,1,0:T(1,128)S(1)} %all_to_all.14), channel_id=1, replica_groups=mesh['elem'=32,'band'=16] {'elem'}, dimensions={0} | all-to-all | bytes 532480 | tf_op jit(solution)/shard_map/all_to_all | solution.py:39
  181.7 0.2 reduce_sum.22
  181.8 0.9 broadcast_in_dim.5
  182.7 3.9 %all-to-all-start.2 = ((f32[32,1,2080]{2,1,0:T(1,128)}), f32[32,1,2080]{2,1,0:T(1,128)S(1)}, u32[]{:S(2)}, u32[]{:S(2)}) async-start(f32[32,1,2080]{2,1,0:T(1,128)} %broadcast_in_dim.5), calls=%async_computation.2 | async-start | bytes 557056 | tf_op jit(solution)/shard_map/all_to_all | solution.py:56
  186.6 22.2 %all-to-all-done.2 = f32[32,1,2080]{2,1,0:T(1,128)S(1)} async-done(((f32[32,1,2080]{2,1,0:T(1,128)}), f32[32,1,2080]{2,1,0:T(1,128)S(1)}, u32[]{:S(2)}, u32[]{:S(2)}) %all-to-all-start.2) | async-done | bytes 266272 | tf_op jit(solution)/shard_map/all_to_all | solution.py:56
  208.8 0.7 reduce.2
  209.4 0.3 slice.126
  209.7 0.2 reshape.69
  209.9 0.1 dynamic_slice.3
  210.0 4.3 %convolution_convert_fusion = bf16[64,2560]{1,0:T(8,128)(2,1)} fusion(bf16[1024,2560]{1,0:T(8,128)(2,1)} %bitcast.87, f32[65,1024]{1,0:T(8,128)S(1)} %slice.126, f32[1024]{0:T(1024)S(1)} %get-tuple-element.18, f32[64]{0:T(128)S(1)} %dynamic_slice.3, s32[64]{0:T(128)S(1)} %iota_add_fusion, f32[1024]{0:T(1024)S(1)} %get-tuple-element.17), kind=kOutput, calls=%fused_computation.1 | convolution fusion | flops 336232448 | bytes 5841920 | tf_op jit(solution)/shard_map/dot_general | solution.py:138
  (23 shorter events, 0.1 us)
Async XLA Ops:
  0.0 19.1 %copy-start = (bf16[16,160,160]{2,1,0:T(8,128)(2,1)S(1)}, bf16[16,160,160]{2,1,0:T(8,128)(2,1)}, u32[]{:S(2)}) copy-start(bf16[16,160,160]{2,1,0:T(8,128)(2,1)} %param.7) | copy-start | bytes 2457604
  0.0 15.0 %copy-start.3 = (s32[16]{0:T(128)S(1)}, s32[16]{0:T(128)}, u32[]{:S(2)}) copy-start(s32[16]{0:T(128)} %param.6) | copy-start | bytes 196
  0.0 15.0 %copy-start.2 = (bf16[16,160,160]{2,1,0:T(8,128)(2,1)S(1)}, bf16[16,160,160]{2,1,0:T(8,128)(2,1)}, u32[]{:S(2)}) copy-start(bf16[16,160,160]{2,1,0:T(8,128)(2,1)} %param.8) | copy-start | bytes 2457604
  2.7 17.1 %collective-permute-start = (bf16[64,1,160]{2,0,1:T(8,128)(2,1)S(1)}, bf16[64,1,160]{2,0,1:T(8,128)(2,1)S(1)}, u32[]{:S(2)}, u32[]{:S(2)}) collective-permute-start(bf16[64,1,160]{2,0,1:T(8,128)(2,1)S(1)} %get-tuple-element.16), channel_id=1, source_target_pairs={{16,0},{32,16},{48,32},{64,48},{80,64},{96,80},{112,96},{128,112},... | collective-permute-start | bytes 61448 | tf_op jit(solution)/shard_map/ppermute | solution.py:27
  15.2 9.8 %collective-permute-start.2 = (bf16[160,160]{1,0:T(8,128)(2,1)S(1)}, bf16[160,160]{1,0:T(8,128)(2,1)S(1)}, u32[]{:S(2)}, u32[]{:S(2)}) collective-permute-start(bf16[160,160]{1,0:T(8,128)(2,1)S(1)} %slice_bitcast_fusion), channel_id=1, source_target_pairs={{0,16},{16,32},{32,48},{48,64},{64,80},{80,96},{96,112},{112,128},... | collective-permute-start | bytes 153608 | tf_op jit(solution)/shard_map/ppermute | solution.py:16
  17.2 7.9 %collective-permute-start.1 = (bf16[64,1,160]{2,0,1:T(8,128)(2,1)S(1)}, bf16[64,1,160]{2,0,1:T(8,128)(2,1)S(1)}, u32[]{:S(2)}, u32[]{:S(2)}) collective-permute-start(bf16[64,1,160]{2,0,1:T(8,128)(2,1)S(1)} %get-tuple-element.15), channel_id=1, source_target_pairs={{0,16},{16,32},{32,48},{48,64},{64,80},{80,96},{96,112},{112,128},... | collective-permute-start | bytes 61448 | tf_op jit(solution)/shard_map/ppermute | solution.py:26
  25.5 6.4 %collective-permute-start.3 = (bf16[64,1,160]{2,0,1:T(8,128)(2,1)S(1)}, bf16[64,1,160]{2,0,1:T(8,128)(2,1)S(1)}, u32[]{:S(2)}, u32[]{:S(2)}) collective-permute-start(bf16[64,1,160]{2,0,1:T(8,128)(2,1)S(1)} %get-tuple-element.14), channel_id=1, source_target_pairs={{16,0},{32,16},{48,32},{64,48},{80,64},{96,80},{112,96},{128,112},... | collective-permute-start | bytes 61448 | tf_op jit(solution)/shard_map/ppermute | solution.py:27
  30.0 7.9 %collective-permute-start.4 = (bf16[64,1,160]{2,0,1:T(8,128)(2,1)S(1)}, bf16[64,1,160]{2,0,1:T(8,128)(2,1)S(1)}, u32[]{:S(2)}, u32[]{:S(2)}) collective-permute-start(bf16[64,1,160]{2,0,1:T(8,128)(2,1)S(1)} %get-tuple-element.13), channel_id=1, source_target_pairs={{0,16},{16,32},{32,48},{48,64},{64,80},{80,96},{96,112},{112,128},... | collective-permute-start | bytes 61448 | tf_op jit(solution)/shard_map/ppermute | solution.py:26
  38.5 6.4 %collective-permute-start.5 = (bf16[64,1,160]{2,0,1:T(8,128)(2,1)S(1)}, bf16[64,1,160]{2,0,1:T(8,128)(2,1)S(1)}, u32[]{:S(2)}, u32[]{:S(2)}) collective-permute-start(bf16[64,1,160]{2,0,1:T(8,128)(2,1)S(1)} %get-tuple-element.12), channel_id=1, source_target_pairs={{16,0},{32,16},{48,32},{64,48},{80,64},{96,80},{112,96},{128,112},... | collective-permute-start | bytes 61448 | tf_op jit(solution)/shard_map/ppermute | solution.py:27
  40.9 7.9 %collective-permute-start.6 = (bf16[64,1,160]{2,0,1:T(8,128)(2,1)S(1)}, bf16[64,1,160]{2,0,1:T(8,128)(2,1)S(1)}, u32[]{:S(2)}, u32[]{:S(2)}) collective-permute-start(bf16[64,1,160]{2,0,1:T(8,128)(2,1)S(1)} %get-tuple-element.11), channel_id=1, source_target_pairs={{0,16},{16,32},{32,48},{48,64},{64,80},{80,96},{96,112},{112,128},... | collective-permute-start | bytes 61448 | tf_op jit(solution)/shard_map/ppermute | solution.py:26
  49.4 6.4 %collective-permute-start.7 = (bf16[64,1,160]{2,0,1:T(8,128)(2,1)S(1)}, bf16[64,1,160]{2,0,1:T(8,128)(2,1)S(1)}, u32[]{:S(2)}, u32[]{:S(2)}) collective-permute-start(bf16[64,1,160]{2,0,1:T(8,128)(2,1)S(1)} %get-tuple-element.10), channel_id=1, source_target_pairs={{16,0},{32,16},{48,32},{64,48},{80,64},{96,80},{112,96},{128,112},... | collective-permute-start | bytes 61448 | tf_op jit(solution)/shard_map/ppermute | solution.py:27
  51.9 7.9 %collective-permute-start.8 = (bf16[64,1,160]{2,0,1:T(8,128)(2,1)S(1)}, bf16[64,1,160]{2,0,1:T(8,128)(2,1)S(1)}, u32[]{:S(2)}, u32[]{:S(2)}) collective-permute-start(bf16[64,1,160]{2,0,1:T(8,128)(2,1)S(1)} %get-tuple-element.9), channel_id=1, source_target_pairs={{0,16},{16,32},{32,48},{48,64},{64,80},{80,96},{96,112},{112,128},... | collective-permute-start | bytes 61448 | tf_op jit(solution)/shard_map/ppermute | solution.py:26
  60.3 6.4 %collective-permute-start.9 = (bf16[64,1,160]{2,0,1:T(8,128)(2,1)S(1)}, bf16[64,1,160]{2,0,1:T(8,128)(2,1)S(1)}, u32[]{:S(2)}, u32[]{:S(2)}) collective-permute-start(bf16[64,1,160]{2,0,1:T(8,128)(2,1)S(1)} %get-tuple-element.8), channel_id=1, source_target_pairs={{16,0},{32,16},{48,32},{64,48},{80,64},{96,80},{112,96},{128,112},... | collective-permute-start | bytes 61448 | tf_op jit(solution)/shard_map/ppermute | solution.py:27
  62.8 7.9 %collective-permute-start.10 = (bf16[64,1,160]{2,0,1:T(8,128)(2,1)S(1)}, bf16[64,1,160]{2,0,1:T(8,128)(2,1)S(1)}, u32[]{:S(2)}, u32[]{:S(2)}) collective-permute-start(bf16[64,1,160]{2,0,1:T(8,128)(2,1)S(1)} %get-tuple-element.7), channel_id=1, source_target_pairs={{0,16},{16,32},{32,48},{48,64},{64,80},{80,96},{96,112},{112,128},... | collective-permute-start | bytes 61448 | tf_op jit(solution)/shard_map/ppermute | solution.py:26
  71.2 6.4 %collective-permute-start.11 = (bf16[64,1,160]{2,0,1:T(8,128)(2,1)S(1)}, bf16[64,1,160]{2,0,1:T(8,128)(2,1)S(1)}, u32[]{:S(2)}, u32[]{:S(2)}) collective-permute-start(bf16[64,1,160]{2,0,1:T(8,128)(2,1)S(1)} %get-tuple-element.6), channel_id=1, source_target_pairs={{16,0},{32,16},{48,32},{64,48},{80,64},{96,80},{112,96},{128,112},... | collective-permute-start | bytes 61448 | tf_op jit(solution)/shard_map/ppermute | solution.py:27
  73.7 7.9 %collective-permute-start.12 = (bf16[64,1,160]{2,0,1:T(8,128)(2,1)S(1)}, bf16[64,1,160]{2,0,1:T(8,128)(2,1)S(1)}, u32[]{:S(2)}, u32[]{:S(2)}) collective-permute-start(bf16[64,1,160]{2,0,1:T(8,128)(2,1)S(1)} %get-tuple-element.5), channel_id=1, source_target_pairs={{0,16},{16,32},{32,48},{48,64},{64,80},{80,96},{96,112},{112,128},... | collective-permute-start | bytes 61448 | tf_op jit(solution)/shard_map/ppermute | solution.py:26
  151.1 2.3 %copy-start.1 = (bf16[16,64,2560]{2,1,0:T(8,128)(2,1)}, bf16[16,64,2560]{2,1,0:T(8,128)(2,1)S(1)}, u32[]{:S(2)}) copy-start(bf16[16,64,2560]{2,1,0:T(8,128)(2,1)S(1)} %all_to_all.20) | copy-start | bytes 15728644
  182.7 26.1 %all-to-all-start.2 = ((f32[32,1,2080]{2,1,0:T(1,128)}), f32[32,1,2080]{2,1,0:T(1,128)S(1)}, u32[]{:S(2)}, u32[]{:S(2)}) async-start(f32[32,1,2080]{2,1,0:T(1,128)} %broadcast_in_dim.5), calls=%async_computation.2 | async-start | bytes 557056 | tf_op jit(solution)/shard_map/all_to_all | solution.py:56
